TPU v7x, 32 devices: a whole 2x2x4 slice. The times are simulated.
32 devices in a mesh: fsdp: 8 (over z, x), head: 2 (over core), tensor: 2 (over y).
Axes of the slice: x: 2, y: 2, z: 4, core: 2. Of those that a mesh axis runs over, the one named last changes fastest.
Arguments:
- block_in: bfloat16 [4096, 1024], P('fsdp'), may hold values from -6 to 6
- cotangent: bfloat16 [4096, 1024], P('fsdp'), may hold values from -6 to 6
- norm_gain: float32 [1024], replicated, may hold values from 0.5 to 1.5
- w_x: bfloat16 [1024, 32, 64], P('fsdp', 'head', 'tensor'), may hold values from -0.1875 to 0.1875
- w_z: bfloat16 [1024, 32, 64], P('fsdp', 'head', 'tensor'), may hold values from -0.1875 to 0.1875
- w_bc: bfloat16 [1024, 2, 128], P('fsdp'), may hold values from -0.1875 to 0.1875
- w_dt: bfloat16 [1024, 32], P('fsdp', 'head'), may hold values from -0.1875 to 0.1875
- conv_x: float32 [32, 64, 4], P('head', 'tensor'), may hold values from -3 to 3
- conv_bc: float32 [2, 128, 4], replicated, may hold values from -3 to 3
- dt_bias: float32 [32], P('head'), may hold values from -6 to -2
- a_log: float32 [32], P('head'), may hold values from -1.5 to 0.5
- skip: float32 [32], P('head'), may hold values from 0.5 to 1.5
- gate_gain: float32 [32, 64], P('head', 'tensor'), may hold values from 0.5 to 1.5
- w_out: bfloat16 [32, 64, 1024], P('head', 'tensor', 'fsdp'), may hold values from -0.125 to 0.125
Outputs:
- block_out: bfloat16 [4096, 1024], P('fsdp')
- grad_in: float32 [4096, 1024], P('fsdp')
- grad_norm_gain: float32 [1024], replicated
- grad_w_x: float32 [1024, 32, 64], P('fsdp', 'head', 'tensor')
- grad_w_z: float32 [1024, 32, 64], P('fsdp', 'head', 'tensor')
- grad_w_bc: float32 [1024, 2, 128], P('fsdp')
- grad_w_dt: float32 [1024, 32], P('fsdp', 'head')
- grad_conv_x: float32 [32, 64, 4], P('head', 'tensor')
- grad_conv_bc: float32 [2, 128, 4], replicated
- grad_dt_bias: float32 [32], P('head')
- grad_a_log: float32 [32], P('head')
- grad_skip: float32 [32], P('head')
- grad_gate_gain: float32 [32, 64], P('head', 'tensor')
- grad_w_out: float32 [32, 64, 1024], P('head', 'tensor', 'fsdp')
All inputs are finite; a program needn't handle non-finite values.
Results may differ from a plain program's by a relative error of at most 0.011.
Values may be sent and summed in bfloat16 or wider, within the bound.
A program may use at most 128 MiB of HBM per device.

v0:
```python
from functools import partial
import jax
import jax.numpy as jnp
from jax import lax
from jax.sharding import PartitionSpec as P

SPAN = 256
EPSILON = 1e-05
PRECISE = lax.Precision.HIGHEST


def causal_conv(signal, kernel):
    taps = kernel.shape[1]
    length = signal.shape[0]
    padded = jnp.pad(signal, ((taps - 1, 0), (0, 0)))
    total = jnp.zeros_like(signal)
    for offset in range(taps):
        total = total + padded[offset : offset + length] * kernel[:, offset]
    return total


def conv_silu(signal, kernel):
    return jax.nn.silu(causal_conv(signal, kernel))


def silu_slope(value):
    sigma = jax.nn.sigmoid(value)
    return sigma * (1.0 + value * (1.0 - sigma))


def scan_spans(values, step_size, rate, b_maps, c_maps, block):
    length, head_count, channels = values.shape
    blocks = length // block
    logs = (step_size * rate).reshape(blocks, block, head_count)
    cums = jnp.cumsum(logs, axis=1)
    x_blocks = values.reshape(blocks, block, head_count, channels)
    dt_blocks = step_size.reshape(blocks, block, head_count)
    b_blocks = b_maps.reshape(blocks, block, -1)
    c_blocks = c_maps.reshape(blocks, block, -1)
    scores = jnp.einsum("cln,csn->cls", c_blocks, b_blocks, precision=PRECISE)
    causal = (jnp.arange(block)[:, None] >= jnp.arange(block)[None, :])[None, :, :, None]
    gaps = cums[:, :, None, :] - cums[:, None, :, :]
    decays = jnp.where(causal, jnp.exp(jnp.where(causal, gaps, 0.0)), 0.0)
    mixing = scores[..., None] * decays * dt_blocks[:, None, :, :]
    intra_part = jnp.einsum("clsh,cshp->clhp", mixing, x_blocks, precision=PRECISE)
    to_end = jnp.exp(cums[:, -1:, :] - cums) * dt_blocks
    states = jnp.einsum("csh,csn,cshp->chpn", to_end, b_blocks, x_blocks, precision=PRECISE)
    whole_decay = jnp.exp(cums[:, -1, :])
    carried = []
    running = jnp.zeros_like(states[0])
    for position in range(blocks):
        carried.append(running)
        running = running * whole_decay[position][:, None, None] + states[position]
    entering = jnp.stack(carried)
    inter_part = jnp.einsum(
        "cln,clh,chpn->clhp", c_blocks, jnp.exp(cums), entering, precision=PRECISE
    )
    return (intra_part + inter_part).reshape(length, head_count, channels)


def mixer(values, dt_raw, dt_bias, a_log, skip, b_maps, c_maps, block):
    step_size = jax.nn.softplus(dt_raw + dt_bias)
    rate = -jnp.exp(a_log)
    return scan_spans(values, step_size, rate, b_maps, c_maps, block) + skip[:, None] * values


def on_device(
    block_in,
    cotangent,
    norm_gain,
    w_x,
    w_z,
    w_bc,
    w_dt,
    conv_x,
    conv_bc,
    dt_bias,
    a_log,
    skip,
    gate_gain,
    w_out,
):
    length, model_width = block_in.shape
    head_count, head_width, taps = conv_x.shape
    state_size = conv_bc.shape[1]
    inner_width = head_count * head_width
    group_count = lax.axis_size("head") * lax.axis_size("tensor")
    full_inner = inner_width * group_count
    weights = (w_x, w_z, w_bc, w_dt, w_out)
    gathered = (
        lax.all_gather(weights[0], "fsdp", axis=0, tiled=True),
        lax.all_gather(weights[1], "fsdp", axis=0, tiled=True),
        lax.all_gather(weights[2], "fsdp", axis=0, tiled=True),
        lax.all_gather(weights[3], "fsdp", axis=0, tiled=True),
        lax.all_gather(weights[4], "fsdp", axis=2, tiled=True),
    )
    weight_x = gathered[0].reshape(model_width, inner_width)
    weight_z = gathered[1].reshape(model_width, inner_width)
    weight_bc = gathered[2].reshape(model_width, 2 * state_size)
    weight_dt = gathered[3]
    weight_out = gathered[4].reshape(inner_width, model_width)
    kernel_x = conv_x.reshape(inner_width, taps)
    kernel_bc = conv_bc.reshape(2 * state_size, taps)
    gain_flat = gate_gain.reshape(inner_width)
    features = block_in.astype(jnp.float32)
    scale_in = lax.rsqrt(jnp.mean(features * features, axis=1, keepdims=True) + EPSILON)
    normed = (features * scale_in * norm_gain).astype(jnp.bfloat16)
    x_raw = jnp.dot(normed, weight_x, preferred_element_type=jnp.float32)
    z_raw = jnp.dot(normed, weight_z, preferred_element_type=jnp.float32)
    bc_raw = jnp.dot(normed, weight_bc, preferred_element_type=jnp.float32)
    dt_raw = jnp.dot(normed, weight_dt, preferred_element_type=jnp.float32)
    x_act = conv_silu(x_raw, kernel_x).astype(jnp.bfloat16)
    bc_act = conv_silu(bc_raw, kernel_bc).astype(jnp.bfloat16)
    values = x_act.astype(jnp.float32).reshape(length, head_count, head_width)
    b_maps = bc_act[:, :state_size].astype(jnp.float32)
    c_maps = bc_act[:, state_size:].astype(jnp.float32)
    mixed = mixer(values, dt_raw, dt_bias, a_log, skip, b_maps, c_maps, SPAN).reshape(
        length, inner_width
    )
    gated = mixed * jax.nn.silu(z_raw)
    square_sum = lax.psum(jnp.sum(gated * gated, axis=1), ("head", "tensor"))
    scale_out = lax.rsqrt(square_sum / full_inner + EPSILON)[:, None]
    normed_out = (gated * scale_out * gain_flat).astype(jnp.bfloat16)
    partial_out = jnp.dot(normed_out, weight_out, preferred_element_type=jnp.float32)
    summed = lax.psum(partial_out, ("head", "tensor"))
    block_out = (summed + features).astype(jnp.bfloat16)
    again = (
        lax.all_gather(weights[0], "fsdp", axis=0, tiled=True),
        lax.all_gather(weights[1], "fsdp", axis=0, tiled=True),
        lax.all_gather(weights[2], "fsdp", axis=0, tiled=True),
        lax.all_gather(weights[3], "fsdp", axis=0, tiled=True),
        lax.all_gather(weights[4], "fsdp", axis=2, tiled=True),
    )
    back_x = again[0].reshape(model_width, inner_width)
    back_z = again[1].reshape(model_width, inner_width)
    back_bc = again[2].reshape(model_width, 2 * state_size)
    back_dt = again[3]
    back_out = again[4].reshape(inner_width, model_width)
    upstream = cotangent.astype(jnp.float32)
    d_normed_out = jnp.dot(cotangent, back_out.T, preferred_element_type=jnp.float32)
    g_w_out = jnp.dot(normed_out.T, cotangent, preferred_element_type=jnp.float32)
    g_gate_gain = jnp.sum(d_normed_out * gated * scale_out, axis=0)
    d_hat = d_normed_out * gain_flat
    inner_sum = lax.psum(jnp.sum(d_hat * gated, axis=1), ("head", "tensor"))[:, None]
    d_gated = scale_out * d_hat - gated * scale_out**3 * inner_sum / full_inner
    d_mixed = d_gated * jax.nn.silu(z_raw)
    d_z = (d_gated * mixed * silu_slope(z_raw)).astype(jnp.bfloat16)
    _, pullback = jax.vjp(
        partial(mixer, block=SPAN), values, dt_raw, dt_bias, a_log, skip, b_maps, c_maps
    )
    d_xs, d_dt, g_dt_bias, g_a_log, g_skip, d_b, d_c = pullback(
        d_mixed.reshape(length, head_count, head_width)
    )
    d_dt, g_dt_bias, g_a_log, g_skip = lax.psum((d_dt, g_dt_bias, g_a_log, g_skip), "tensor")
    d_bc = lax.psum(jnp.concatenate([d_b, d_c], axis=1), ("head", "tensor"))
    _, pull_x = jax.vjp(conv_silu, x_raw, kernel_x)
    d_x_raw, g_conv_x = pull_x(d_xs.reshape(length, inner_width))
    _, pull_bc = jax.vjp(conv_silu, bc_raw, kernel_bc)
    d_bc_raw, g_conv_bc = pull_bc(d_bc)
    d_x_b = d_x_raw.astype(jnp.bfloat16)
    d_bc_b = d_bc_raw.astype(jnp.bfloat16)
    d_dt_b = d_dt.astype(jnp.bfloat16)
    g_w_x = jnp.dot(normed.T, d_x_b, preferred_element_type=jnp.float32)
    g_w_z = jnp.dot(normed.T, d_z, preferred_element_type=jnp.float32)
    g_w_bc = jnp.dot(normed.T, d_bc_b, preferred_element_type=jnp.float32)
    g_w_dt = jnp.dot(normed.T, d_dt_b, preferred_element_type=jnp.float32)
    local_part = (
        jnp.dot(d_x_b, back_x.T, preferred_element_type=jnp.float32)
        + jnp.dot(d_z, back_z.T, preferred_element_type=jnp.float32)
        + jnp.dot(d_dt_b, back_dt.T, preferred_element_type=jnp.float32)
        * (1.0 / lax.axis_size("tensor"))
    )
    d_normed = lax.psum(local_part, ("head", "tensor")) + jnp.dot(
        d_bc_b, back_bc.T, preferred_element_type=jnp.float32
    )
    g_norm_gain = jnp.sum(d_normed * features * scale_in, axis=0)
    d_in_hat = d_normed * norm_gain
    grad_in = (
        scale_in * d_in_hat
        - features * scale_in**3 * jnp.mean(d_in_hat * features, axis=1, keepdims=True)
        + upstream
    )
    big_grads = (
        lax.psum_scatter(
            g_w_x.reshape(model_width, head_count, head_width),
            "fsdp",
            scatter_dimension=0,
            tiled=True,
        ),
        lax.psum_scatter(
            g_w_z.reshape(model_width, head_count, head_width),
            "fsdp",
            scatter_dimension=0,
            tiled=True,
        ),
        lax.psum_scatter(g_w_bc, "fsdp", scatter_dimension=0, tiled=True),
        lax.psum_scatter(g_w_dt, "fsdp", scatter_dimension=0, tiled=True),
        lax.psum_scatter(
            g_w_out.reshape(head_count, head_width, model_width),
            "fsdp",
            scatter_dimension=2,
            tiled=True,
        ),
    )
    owned_bc = big_grads[2].reshape(-1, 2, state_size)
    small = lax.psum(
        (
            g_norm_gain,
            g_conv_x.reshape(head_count, head_width, taps),
            g_conv_bc.reshape(2, state_size, taps),
            g_dt_bias,
            g_a_log,
            g_skip,
            g_gate_gain.reshape(head_count, head_width),
        ),
        "fsdp",
    )
    return (
        block_out,
        grad_in,
        small[0],
        big_grads[0],
        big_grads[1],
        owned_bc,
        big_grads[3],
        small[1],
        small[2],
        small[3],
        small[4],
        small[5],
        small[6],
        big_grads[4],
    )


def solution(mesh):
    return jax.shard_map(
        on_device,
        mesh=mesh,
        in_specs=(
            P("fsdp", None),
            P("fsdp", None),
            P(),
            P("fsdp", "head", "tensor"),
            P("fsdp", "head", "tensor"),
            P("fsdp", None, None),
            P("fsdp", "head"),
            P("head", "tensor", None),
            P(),
            P("head"),
            P("head"),
            P("head"),
            P("head", "tensor"),
            P("head", "tensor", "fsdp"),
        ),
        out_specs=(
            P("fsdp", None),
            P("fsdp", None),
            P(),
            P("fsdp", "head", "tensor"),
            P("fsdp", "head", "tensor"),
            P("fsdp", None, None),
            P("fsdp", "head"),
            P("head", "tensor", None),
            P(),
            P("head"),
            P("head"),
            P("head"),
            P("head", "tensor"),
            P("head", "tensor", "fsdp"),
        ),
        check_vma=False,
    )
```

profile of v0, /device:TPU:0, one launch (start us, length us, event | category | flops | bytes accessed | tf_op | source)
XLA Modules:
  0.0 668.9 jit_solution(9409954152697508148)
XLA Ops:
  13.0 28.3 %all_gather.22 = bf16[1024,16]{0,1:T(8,128)(2,1)S(1)} all-gather(bf16[128,16]{0,1:T(8,128)(2,1)} %param.20), channel_id=1, replica_groups=mesh['fsdp'=8,'head'=2,'tensor'=2] {'fsdp'}, dimensions={0}, use_global_device_ids=true | all-gather | bytes 36864 | tf_op jit(solution)/shard_map/all_gather | solution.py:94
  48.1 32.0 %all_gather.21 = bf16[1024,2,128]{2,1,0:T(2,128)(2,1)S(1)} all-gather(bf16[128,2,128]{2,1,0:T(2,128)(2,1)S(1)} %copy-done.27), channel_id=1, replica_groups=mesh['fsdp'=8,'head'=2,'tensor'=2] {'fsdp'}, dimensions={0}, use_global_device_ids=true | all-gather | bytes 589824 | tf_op jit(solution)/shard_map/all_gather | solution.py:93
  90.0 6.3 fusion.38
  98.5 3.5 multiply_reduce_fusion.9
  102.1 7.9 %psum.112 = f32[512]{0:T(512)S(1)} all-reduce(f32[512]{0:T(512)S(1)} %get-tuple-element.106), channel_id=1, replica_groups=mesh['fsdp'=8,'head'=2,'tensor'=2] {'head','tensor'}, use_global_device_ids=true, to_apply=%region_4.5 | all-reduce | flops 512 | bytes 4096 | tf_op jit(solution)/shard_map/psum | solution.py:121
  110.0 25.5 %all-gather.8.cloned.1.call-done = bf16[16,32,1024]{2,1,0:T(8,128)(2,1)} async-done(((bf16[16,32,128]{2,1,0:T(8,128)(2,1)}), bf16[16,32,1024]{2,1,0:T(8,128)(2,1)}) %all-gather.8.cloned.1.call-update) | async-done | bytes 1048592 | tf_op jit(solution)/shard_map/all_gather | solution.py:95
  135.5 3.9 multiply_reduce_fusion.3
  139.4 7.5 %psum.114 = f32[512]{0:T(512)S(1)} all-reduce(f32[512]{0:T(512)S(1)} %get-tuple-element.77), channel_id=1, replica_groups=mesh['fsdp'=8,'head'=2,'tensor'=2] {'head','tensor'}, use_global_device_ids=true, to_apply=%region_7.8 | all-reduce | flops 512 | bytes 4096 | tf_op jit(solution)/shard_map/psum | solution.py:144
  146.9 4.2 fusion.45
  164.0 11.4 %fusion.9 = (f32[2,256,16]{1,2,0:T(8,128)}, f32[2,256,16]{1,2,0:T(8,128)}, f32[2,256,16]{1,2,0:T(8,128)}, f32[2,256,256]{2,1,0:T(8,128)}) fusion(f32[2,256,16]{1,2,0:T(8,128)S(1)} %bitcast.241, f32[2,256,16]{1,2,0:T(8,128)S(1)} %copy-done.26, f32[2,256,256]{2,1,0:T(8,128)S(1)} %copy-done.20, pred[256,256]{1,0:T(8,128)(4,1)S(1)} %copy-done.29, ...), kind=kOutput, calls=%fused_computation.18 | convolution fusion | flops 836608000 | bytes 2850816 | tf_op jit(solution)/shard_map/transpose(jvp(clsh,cshp->clhp))/dot_general | solution.py:45
  175.5 8.0 %fusion.41 = f32[2,256,16,32]{1,3,2,0:T(8,128)} fusion(f32[2,256,16]{1,2,0:T(8,128)S(1)} %bitcast.242, f32[2,256,16]{1,2,0:T(8,128)S(1)} %copy-done.26, f32[2,256,256]{2,1,0:T(8,128)S(1)} %copy-done.20, pred[256,256]{1,0:T(8,128)(4,1)S(1)} %copy-done.29, f32[2,256,16,32]{1,3,2,0:T(8,128)S(1)} %fusion.58, f32[2,16,32,256]{3,0,2,1:T(2,128)S(1)} %bitcast.207, ...), kind=kOutput, calls=%fused_computation.48 | convolution fusion | flops 816316416 | bytes 3833856 | tf_op jit(solution)/shard_map/transpose(jvp(clsh,cshp->clhp))/dot_general | solution.py:45
  199.9 5.0 reduce-window.16
  205.3 3.6 fusion.118
  214.6 8.2 %all-reduce.25 = (bf16[512,16]{0,1:T(8,128)(2,1)S(1)}, f32[16]{0:T(128)S(1)}, f32[16]{0:T(128)S(1)}, f32[16]{0:T(128)S(1)}) all-reduce(f32[512,16]{0,1:T(8,128)S(1)} %get-tuple-element.105, f32[16]{0:T(128)S(1)} %get-tuple-element.104, f32[16]{0:T(128)S(1)} %negate_multiply_fusion, ...), channel_id=1, replica_groups=mesh['fsdp'=8,'head'=2,'tensor'=2] {'tensor'}, use_global_device_ids=true, to_apply=%region_15.16 | all-reduce | flops 8240 | bytes 49536 | tf_op jit(solution)/shard_map/psum | solution.py:154
  222.8 4.0 multiply_add_fusion
  227.0 92.6 %all-reduce.28.cloned.1.call-done = (f32[512,1024]{1,0:T(8,128)}, f32[512,1024]{1,0:T(8,128)}, f32[512,256]{1,0:T(8,128)}) async-done(((f32[512,1024]{1,0:T(8,128)}, f32[512,1024]{1,0:T(8,128)}, f32[512,256]{1,0:T(8,128)}), (f32[512,1024]{1,0:T(8,128)}, f32[512,1024]{1,0:T(8,128)}, f32[512,256]{1,0:T(8,128)})) %all-reduce.28.cloned.1.call-update) | async-done | bytes 4718608 | tf_op jit(solution)/shard_map/psum | solution.py:125
  324.7 3.4 fusion.92
  336.5 38.1 %all-reduce.23 = (f32[1024]{0:T(1024)}, f32[16,32,4]{1,0,2:T(8,128)S(1)}, f32[2,128,4]{1,2,0:T(4,128)}, f32[16]{0:T(128)}, f32[16]{0:T(128)}, /*index=5*/f32[16]{0:T(128)}, f32[16,32]{1,0:T(8,128)}) all-reduce(f32[1024]{0:T(1024)S(1)} %get-tuple-element.74, ...), channel_id=1, replica_groups=mesh['fsdp'=8,'head'=2,'tensor'=2] {'fsdp'}, use_global_device_ids=true, to_apply=%region_21.22 | all-reduce | flops 4656 | bytes 37248 | tf_op jit(solution)/shard_map/psum | solution.py:206
  375.3 4.3 fusion.28
  379.6 8.5 %reduce-scatter.10.cloned.1.call-done = f32[128,256]{1,0:T(8,128)} async-done(((f32[1024,256]{1,0:T(8,128)}), f32[128,256]{1,0:T(8,128)}) %reduce-scatter.10.cloned.1.call-update) | async-done | bytes 131088 | tf_op jit(solution)/shard_map/reduce_scatter | solution.py:196
  389.7 55.8 %reduce-scatter.12.cloned.1.call-done = f32[128,16]{0,1:T(8,128)} async-done(((f32[1024,16]{0,1:T(8,128)}), f32[128,16]{0,1:T(8,128)}) %reduce-scatter.12.cloned.1.call-update) | async-done | bytes 8208 | tf_op jit(solution)/shard_map/reduce_scatter | solution.py:197
  445.5 72.4 %reduce-scatter.14.cloned.1.call-done = f32[16,32,128]{2,1,0:T(8,128)} async-done(((f32[16,32,1024]{2,1,0:T(8,128)}), f32[16,32,128]{2,1,0:T(8,128)}) %reduce-scatter.14.cloned.1.call-update) | async-done | bytes 262160 | tf_op jit(solution)/shard_map/reduce_scatter | solution.py:198
  517.9 72.0 %reduce-scatter.8.cloned.1.call-done = f32[128,16,32]{0,2,1:T(8,128)} async-done(((f32[1024,16,32]{0,2,1:T(8,128)}), f32[128,16,32]{0,2,1:T(8,128)}) %reduce-scatter.8.cloned.1.call-update) | async-done | bytes 262160 | tf_op jit(solution)/shard_map/reduce_scatter | solution.py:190
  590.0 72.1 %reduce-scatter.6.cloned.1.call-done = f32[128,16,32]{0,2,1:T(8,128)} async-done(((f32[1024,16,32]{0,2,1:T(8,128)}), f32[128,16,32]{0,2,1:T(8,128)}) %reduce-scatter.6.cloned.1.call-update) | async-done | bytes 262160 | tf_op jit(solution)/shard_map/reduce_scatter | solution.py:184
  (261 shorter events, 75.1 us)
Async XLA Ops:
  7.2 40.2 %copy-start.45 = (f32[16,32,4]{1,2,0:T(4,128)S(1)}, f32[16,32,4]{1,2,0:T(4,128)}, u32[]{:S(2)}) copy-start(f32[16,32,4]{1,2,0:T(4,128)} %param.21) | copy-start | bytes 24580
  7.2 40.9 %copy-start.27 = (bf16[128,2,128]{2,1,0:T(2,128)(2,1)S(1)}, bf16[128,2,128]{2,1,0:T(2,128)(2,1)}, u32[]{:S(2)}) copy-start(bf16[128,2,128]{2,1,0:T(2,128)(2,1)} %param.19) | copy-start | bytes 196612
  7.2 75.6 %all-gather.4.cloned.1.call-start = ((), (), s32[]{:S(2)}) async-start(), calls=%async_computation.5 | async-start | bytes 1179648 | tf_op jit(solution)/shard_map/all_gather | solution.py:91
  8.0 90.6 %all-gather.6.cloned.1.call-start = ((), (), s32[]{:S(2)}) async-start(), calls=%async_computation.6 | async-start | bytes 1179648 | tf_op jit(solution)/shard_map/all_gather | solution.py:92
  8.7 126.8 %all-gather.8.cloned.1.call-start = ((), (), s32[]{:S(2)}) async-start(), calls=%async_computation.7 | async-start | bytes 1179648 | tf_op jit(solution)/shard_map/all_gather | solution.py:95
  9.4 310.1 %all-reduce.28.cloned.1.call-start = ((), (), s32[]{:S(2)}) async-start(), calls=%async_computation.13 | async-start | bytes 9437184 | tf_op jit(solution)/shard_map/psum | solution.py:125
  10.8 70.1 %copy-start = (bf16[512,1024]{1,0:T(8,128)(2,1)S(1)}, bf16[512,1024]{1,0:T(8,128)(2,1)}, u32[]{:S(2)}) copy-start(bf16[512,1024]{1,0:T(8,128)(2,1)} %param.14) | copy-start | bytes 3145732
  10.8 70.1 %copy-start.30 = (f32[1024]{0:T(1024)S(1)}, f32[1024]{0:T(1024)}, u32[]{:S(2)}) copy-start(f32[1024]{0:T(1024)} %param.16) | copy-start | bytes 12292
  13.0 85.6 %copy-start.32 = (f32[512]{0:T(512)}, f32[512]{0:T(512)S(1)}, u32[]{:S(2)}) copy-start(f32[512]{0:T(512)S(1)} %get-tuple-element.141) | copy-start | bytes 6148
  45.0 44.9 %copy-start.25 = (f32[2,256,16]{1,2,0:T(8,128)}, f32[2,256,16]{1,2,0:T(8,128)S(1)}, u32[]{:S(2)}) copy-start(f32[2,256,16]{1,2,0:T(8,128)S(1)} %bitcast_bitcast_fusion.1) | copy-start | bytes 98308
  45.2 143.0 %copy-start.36 = (f32[2,16]{1,0:T(2,128)}, f32[2,16]{1,0:T(2,128)S(1)}, u32[]{:S(2)}) copy-start(f32[2,16]{1,0:T(2,128)S(1)} %slice_reduce_fusion.2) | copy-start | bytes 388
  46.6 137.8 %copy-start.38 = (f32[512]{0:T(512)}, f32[512]{0:T(512)S(1)}, u32[]{:S(2)}) copy-start(f32[512]{0:T(512)S(1)} %mul.547) | copy-start | bytes 6148
  110.0 74.5 %copy-start.40 = (f32[512]{0:T(512)}, f32[512]{0:T(512)S(1)}, u32[]{:S(2)}) copy-start(f32[512]{0:T(512)S(1)} %get-tuple-element.143) | copy-start | bytes 6148
  226.8 92.7 %copy-start.13 = (f32[512,256]{1,0:T(8,128)S(1)}, f32[512,256]{1,0:T(8,128)}, u32[]{:S(2)}) copy-start(f32[512,256]{1,0:T(8,128)} %copy-done.12) | copy-start | bytes 1572868
  226.9 94.3 %copy-start.61 = (f32[256,1]{0,1:T(1,128)S(1)}, f32[256,1]{0,1:T(1,128)}, u32[]{:S(2)}) copy-start(f32[256,1]{0,1:T(1,128)} %copy-done.60) | copy-start | bytes 3076
  226.9 94.3 %copy-start.63 = (f32[256,1]{0,1:T(1,128)S(1)}, f32[256,1]{0,1:T(1,128)}, u32[]{:S(2)}) copy-start(f32[256,1]{0,1:T(1,128)} %copy-done.62) | copy-start | bytes 3076
  226.9 94.3 %copy-start.65 = (f32[256,1]{0,1:T(1,128)S(1)}, f32[256,1]{0,1:T(1,128)}, u32[]{:S(2)}) copy-start(f32[256,1]{0,1:T(1,128)} %copy-done.64) | copy-start | bytes 3076
  226.9 94.3 %copy-start.67 = (f32[256,1]{0,1:T(1,128)S(1)}, f32[256,1]{0,1:T(1,128)}, u32[]{:S(2)}) copy-start(f32[256,1]{0,1:T(1,128)} %copy-done.66) | copy-start | bytes 3076
  226.9 161.2 %reduce-scatter.10.cloned.1.call-start = ((), (), s32[]{:S(2)}) async-start(), calls=%async_computation.10 | async-start | bytes 1179648 | tf_op jit(solution)/shard_map/reduce_scatter | solution.py:196
  323.5 122.0 %reduce-scatter.12.cloned.1.call-start = ((), (), s32[]{:S(2)}) async-start(), calls=%async_computation.11 | async-start | bytes 73728 | tf_op jit(solution)/shard_map/reduce_scatter | solution.py:197
  324.6 193.3 %reduce-scatter.14.cloned.1.call-start = ((), (), s32[]{:S(2)}) async-start(), calls=%async_computation.12 | async-start | bytes 2359296 | tf_op jit(solution)/shard_map/reduce_scatter | solution.py:198
  328.1 261.9 %reduce-scatter.8.cloned.1.call-start = ((), (), s32[]{:S(2)}) async-start(), calls=%async_computation.9 | async-start | bytes 2359296 | tf_op jit(solution)/shard_map/reduce_scatter | solution.py:190
  331.4 330.7 %reduce-scatter.6.cloned.1.call-start = ((), (), s32[]{:S(2)}) async-start(), calls=%async_computation.8 | async-start | bytes 2359296 | tf_op jit(solution)/shard_map/reduce_scatter | solution.py:184
  333.8 41.4 %copy-start.68 = (f32[512]{0:T(512)S(1)}, f32[512]{0:T(512)}, u32[]{:S(2)}) copy-start(f32[512]{0:T(512)} %get-tuple-element.140) | copy-start | bytes 6148
  (62 other events, 661.5 us)
Sparse Core Ops, SparseCore 0:
  10.1 43.5 all-gather.3
  55.8 39.1 all-gather.5
  97.1 38.3 all-gather.7
  227.0 92.4 all-reduce.27
  323.6 64.4 reduce-scatter.9
  391.7 53.8 reduce-scatter.11
  449.6 68.2 reduce-scatter.13
  522.0 67.8 reduce-scatter.7
  594.1 67.9 reduce-scatter.5
where the time goes:
time: 679 us; the launch traced here: 669 us
  waiting for transfers between devices  401 us (59%)
  blocking collectives  122 us (18%)
  matrix products  76.5 us (11%)
  other arithmetic  32.2 us (5%)
  local copies, waits for them, and re-layouts  21.5 us (3%)
  between operations  15 us (2%)
    psum x1, waiting for transfers between devices, on_device(): summed = lax.psum(partial_out, ('head', 'tensor'))  92.6 us
    reduce_scatter x1, waiting for transfers between devices, on_device(): lax.psum_scatter(g_w_out.reshape(head_count, head_width, model_width), 'f...  72.4 us
    reduce_scatter x1, waiting for transfers between devices, on_device(): lax.psum_scatter(g_w_x.reshape(model_width, head_count, head_width), 'fsd...  72.1 us
    reduce_scatter x1, waiting for transfers between devices, on_device(): lax.psum_scatter(g_w_z.reshape(model_width, head_count, head_width), 'fsd...  72 us
    reduce_scatter x1, waiting for transfers between devices, on_device(): lax.psum_scatter(g_w_dt, 'fsdp', scatter_dimension=0, tiled=True)  55.8 us
    psum x1, blocking collectives, on_device(): lax.psum((g_norm_gain, g_conv_x.reshape(head_count, head_width, taps), g_...  38.1 us
    all_gather x1, blocking collectives, on_device(): lax.all_gather(weights[2], 'fsdp', axis=0, tiled=True)  32 us
    all_gather x1, blocking collectives, on_device(): lax.all_gather(weights[3], 'fsdp', axis=0, tiled=True)  28.3 us
  transfers between devices with their start and end apart: 9, of which 7 were waited for; matrix products, arithmetic and copies ran while one was open for 7% of the time, Pallas kernels for 0%

commit v1 on v0

--- a/solution.py
+++ b/solution.py
@@ -122,7 +122,7 @@
     scale_out = lax.rsqrt(square_sum / full_inner + EPSILON)[:, None]
     normed_out = (gated * scale_out * gain_flat).astype(jnp.bfloat16)
     partial_out = jnp.dot(normed_out, weight_out, preferred_element_type=jnp.float32)
-    summed = lax.psum(partial_out, ("head", "tensor"))
+    summed = lax.psum(lax.psum(partial_out, "tensor"), "head")
     block_out = (summed + features).astype(jnp.bfloat16)
     again = (
         lax.all_gather(weights[0], "fsdp", axis=0, tiled=True),

time: 679 us -> 732 us (1.078)
  waiting for transfers between devices: 401 us -> 453 us
    psum x1 -> x3, waiting for transfers between devices: 92.6 us -> 137 us  [the longest x2 82.2 us: on_device(): summed = lax.psum(lax.psum(partial_out, 'tensor'), 'head')]
    reduce_scatter x1, waiting for transfers between devices: 8.55 us -> 16.2 us  [on_device(): lax.psum_scatter(g_w_bc, 'fsdp', scatter_dimension=0, tiled=True)]
  transfers between devices with their start and end apart: 9 -> 11, of which waited for: 7 -> 9; matrix products, arithmetic and copies ran while one was open for 7% -> 8% of each run, Pallas kernels for 0% -> 0%
where the time goes in v1:
time: 732 us; the launch traced here: 721 us
  waiting for transfers between devices  453 us (62%)
  blocking collectives  122 us (17%)
  matrix products  77.8 us (11%)
  other arithmetic  32.3 us (4%)
  local copies, waits for them, and re-layouts  21.1 us (3%)
  between operations  15 us (2%)
    psum x2, waiting for transfers between devices, on_device(): summed = lax.psum(lax.psum(partial_out, 'tensor'), 'head')  82.2 us
    reduce_scatter x1, waiting for transfers between devices, on_device(): lax.psum_scatter(g_w_x.reshape(model_width, head_count, head_width), 'fsd...  72.3 us
    reduce_scatter x1, waiting for transfers between devices, on_device(): lax.psum_scatter(g_w_out.reshape(head_count, head_width, model_width), 'f...  72.1 us
    reduce_scatter x1, waiting for transfers between devices, on_device(): lax.psum_scatter(g_w_z.reshape(model_width, head_count, head_width), 'fsd...  71.8 us
    reduce_scatter x1, waiting for transfers between devices, on_device(): lax.psum_scatter(g_w_dt, 'fsdp', scatter_dimension=0, tiled=True)  55.4 us
    psum x1, waiting for transfers between devices, on_device(): lax.psum(local_part, ('head', 'tensor'))  54.5 us
    psum x1, blocking collectives, on_device(): lax.psum((g_norm_gain, g_conv_x.reshape(head_count, head_width, taps), g_...  38.5 us
    all_gather x1, blocking collectives, on_device(): lax.all_gather(weights[2], 'fsdp', axis=0, tiled=True)  31.8 us
  transfers between devices with their start and end apart: 11, of which 9 were waited for; matrix products, arithmetic and copies ran while one was open for 8% of the time, Pallas kernels for 0%

profile of v1, /device:TPU:0, one launch (start us, length us, event | category | flops | bytes accessed | tf_op | source)
XLA Modules:
  0.0 721.3 jit_solution(16568742767415864660)
XLA Ops:
  13.0 28.3 %all_gather.22 = bf16[1024,16]{0,1:T(8,128)(2,1)S(1)} all-gather(bf16[128,16]{0,1:T(8,128)(2,1)} %param.20), channel_id=1, replica_groups=mesh['fsdp'=8,'head'=2,'tensor'=2] {'fsdp'}, dimensions={0}, use_global_device_ids=true | all-gather | bytes 36864 | tf_op jit(solution)/shard_map/all_gather | solution.py:94
  48.2 31.8 %all_gather.21 = bf16[1024,2,128]{2,1,0:T(2,128)(2,1)S(1)} all-gather(bf16[128,2,128]{2,1,0:T(2,128)(2,1)S(1)} %copy-done.26), channel_id=1, replica_groups=mesh['fsdp'=8,'head'=2,'tensor'=2] {'fsdp'}, dimensions={0}, use_global_device_ids=true | all-gather | bytes 589824 | tf_op jit(solution)/shard_map/all_gather | solution.py:93
  89.8 6.3 fusion.38
  102.0 7.6 %psum.119 = f32[512]{0:T(512)S(1)} all-reduce(f32[512]{0:T(512)S(1)} %get-tuple-element.105), channel_id=1, replica_groups=mesh['fsdp'=8,'head'=2,'tensor'=2] {'head','tensor'}, use_global_device_ids=true, to_apply=%region_4.5 | all-reduce | flops 512 | bytes 4096 | tf_op jit(solution)/shard_map/psum | solution.py:121
  109.6 26.2 %all-gather.8.cloned.1.call-done = bf16[16,32,1024]{2,1,0:T(8,128)(2,1)} async-done(((bf16[16,32,128]{2,1,0:T(8,128)(2,1)}), bf16[16,32,1024]{2,1,0:T(8,128)(2,1)}) %all-gather.8.cloned.1.call-update) | async-done | bytes 1048592 | tf_op jit(solution)/shard_map/all_gather | solution.py:95
  135.8 3.9 multiply_reduce_fusion.3
  139.7 7.5 %psum.122 = f32[512]{0:T(512)S(1)} all-reduce(f32[512]{0:T(512)S(1)} %get-tuple-element.77), channel_id=1, replica_groups=mesh['fsdp'=8,'head'=2,'tensor'=2] {'head','tensor'}, use_global_device_ids=true, to_apply=%region_8.9 | all-reduce | flops 512 | bytes 4096 | tf_op jit(solution)/shard_map/psum | solution.py:144
  147.2 4.3 fusion.45
  164.4 11.4 %fusion.9 = (f32[2,256,16]{1,2,0:T(8,128)}, f32[2,256,16]{1,2,0:T(8,128)}, f32[2,256,16]{1,2,0:T(8,128)}, f32[2,256,256]{2,1,0:T(8,128)}) fusion(f32[2,256,16]{1,2,0:T(8,128)S(1)} %bitcast.241, f32[2,256,16]{1,2,0:T(8,128)S(1)} %copy-done.25, f32[2,256,256]{2,1,0:T(8,128)S(1)} %copy-done.19, pred[256,256]{1,0:T(8,128)(4,1)S(1)} %copy-done.28, ...), kind=kOutput, calls=%fused_computation.18 | convolution fusion | flops 836608000 | bytes 2850816 | tf_op jit(solution)/shard_map/transpose(jvp(clsh,cshp->clhp))/dot_general | solution.py:45
  175.9 8.0 %fusion.41 = f32[2,256,16,32]{1,3,2,0:T(8,128)} fusion(f32[2,256,16]{1,2,0:T(8,128)S(1)} %bitcast.242, f32[2,256,16]{1,2,0:T(8,128)S(1)} %copy-done.25, f32[2,256,256]{2,1,0:T(8,128)S(1)} %copy-done.19, pred[256,256]{1,0:T(8,128)(4,1)S(1)} %copy-done.28, f32[2,256,16,32]{1,3,2,0:T(8,128)S(1)} %fusion.58, f32[2,16,32,256]{3,0,2,1:T(2,128)S(1)} %bitcast.207, ...), kind=kOutput, calls=%fused_computation.48 | convolution fusion | flops 816316416 | bytes 3833856 | tf_op jit(solution)/shard_map/transpose(jvp(clsh,cshp->clhp))/dot_general | solution.py:45
  197.2 5.0 reduce-window.16
  202.7 3.6 fusion.118
  211.9 8.0 %all-reduce.25 = (bf16[512,16]{0,1:T(8,128)(2,1)S(1)}, f32[16]{0:T(128)S(1)}, f32[16]{0:T(128)S(1)}, f32[16]{0:T(128)S(1)}) all-reduce(f32[512,16]{0,1:T(8,128)S(1)} %get-tuple-element.104, f32[16]{0:T(128)S(1)} %get-tuple-element.103, f32[16]{0:T(128)S(1)} %negate_multiply_fusion, ...), channel_id=1, replica_groups=mesh['fsdp'=8,'head'=2,'tensor'=2] {'tensor'}, use_global_device_ids=true, to_apply=%region_16.17 | all-reduce | flops 8240 | bytes 49536 | tf_op jit(solution)/shard_map/psum | solution.py:154
  219.9 4.0 multiply_add_fusion
  228.0 54.5 %all-reduce.34.cloned.1.call-done = (f32[512,1024]{1,0:T(8,128)}, f32[512,256]{1,0:T(8,128)}) async-done(((f32[512,1024]{1,0:T(8,128)}, f32[512,256]{1,0:T(8,128)}), (f32[512,1024]{1,0:T(8,128)}, f32[512,256]{1,0:T(8,128)})) %all-reduce.34.cloned.1.call-update) | async-done | bytes 2621456 | tf_op jit(solution)/shard_map/psum | solution.py:173
  286.5 61.2 %all-reduce.30.cloned.1.call-done = f32[512,1024]{1,0:T(8,128)} async-done(((f32[512,1024]{1,0:T(8,128)}), f32[512,1024]{1,0:T(8,128)}) %all-reduce.30.cloned.1.call-update) | async-done | bytes 2097168 | tf_op jit(solution)/shard_map/psum | solution.py:125
  360.7 38.5 %all-reduce.23 = (f32[1024]{0:T(1024)}, f32[16,32,4]{1,0,2:T(8,128)S(1)}, f32[2,128,4]{1,2,0:T(4,128)}, f32[16]{0:T(128)}, f32[16]{0:T(128)}, /*index=5*/f32[16]{0:T(128)}, f32[16,32]{1,0:T(8,128)}) all-reduce(f32[1024]{0:T(1024)S(1)} %get-tuple-element.74, ...), channel_id=1, replica_groups=mesh['fsdp'=8,'head'=2,'tensor'=2] {'fsdp'}, use_global_device_ids=true, to_apply=%region_22.23 | all-reduce | flops 4656 | bytes 37248 | tf_op jit(solution)/shard_map/psum | solution.py:206
  399.9 16.2 %reduce-scatter.10.cloned.1.call-done = f32[128,256]{1,0:T(8,128)} async-done(((f32[1024,256]{1,0:T(8,128)}), f32[128,256]{1,0:T(8,128)}) %reduce-scatter.10.cloned.1.call-update) | async-done | bytes 131088 | tf_op jit(solution)/shard_map/reduce_scatter | solution.py:196
  417.7 21.0 %all-reduce.32.cloned.1.call-done = f32[512,1024]{1,0:T(8,128)} async-done(((f32[512,1024]{1,0:T(8,128)}), f32[512,1024]{1,0:T(8,128)}) %all-reduce.32.cloned.1.call-update) | async-done | bytes 2097168 | tf_op jit(solution)/shard_map/psum | solution.py:125
  438.6 4.3 fusion.28
  442.9 55.4 %reduce-scatter.12.cloned.1.call-done = f32[128,16]{0,1:T(8,128)} async-done(((f32[1024,16]{0,1:T(8,128)}), f32[128,16]{0,1:T(8,128)}) %reduce-scatter.12.cloned.1.call-update) | async-done | bytes 8208 | tf_op jit(solution)/shard_map/reduce_scatter | solution.py:197
  498.3 72.1 %reduce-scatter.14.cloned.1.call-done = f32[16,32,128]{2,1,0:T(8,128)} async-done(((f32[16,32,1024]{2,1,0:T(8,128)}), f32[16,32,128]{2,1,0:T(8,128)}) %reduce-scatter.14.cloned.1.call-update) | async-done | bytes 262160 | tf_op jit(solution)/shard_map/reduce_scatter | solution.py:198
  570.4 71.8 %reduce-scatter.8.cloned.1.call-done = f32[128,16,32]{0,2,1:T(8,128)} async-done(((f32[1024,16,32]{0,2,1:T(8,128)}), f32[128,16,32]{0,2,1:T(8,128)}) %reduce-scatter.8.cloned.1.call-update) | async-done | bytes 262160 | tf_op jit(solution)/shard_map/reduce_scatter | solution.py:190
  642.2 72.3 %reduce-scatter.6.cloned.1.call-done = f32[128,16,32]{0,2,1:T(8,128)} async-done(((f32[1024,16,32]{0,2,1:T(8,128)}), f32[128,16,32]{0,2,1:T(8,128)}) %reduce-scatter.6.cloned.1.call-update) | async-done | bytes 262160 | tf_op jit(solution)/shard_map/reduce_scatter | solution.py:184
  (267 shorter events, 83.1 us)
Async XLA Ops:
  7.2 40.9 %copy-start.26 = (bf16[128,2,128]{2,1,0:T(2,128)(2,1)S(1)}, bf16[128,2,128]{2,1,0:T(2,128)(2,1)}, u32[]{:S(2)}) copy-start(bf16[128,2,128]{2,1,0:T(2,128)(2,1)} %param.19) | copy-start | bytes 196612
  7.2 75.4 %all-gather.4.cloned.1.call-start = ((), (), s32[]{:S(2)}) async-start(), calls=%async_computation.5 | async-start | bytes 1179648 | tf_op jit(solution)/shard_map/all_gather | solution.py:91
  8.0 90.4 %all-gather.6.cloned.1.call-start = ((), (), s32[]{:S(2)}) async-start(), calls=%async_computation.6 | async-start | bytes 1179648 | tf_op jit(solution)/shard_map/all_gather | solution.py:92
  8.7 127.1 %all-gather.8.cloned.1.call-start = ((), (), s32[]{:S(2)}) async-start(), calls=%async_computation.7 | async-start | bytes 1179648 | tf_op jit(solution)/shard_map/all_gather | solution.py:95
  9.4 273.0 %all-reduce.34.cloned.1.call-start = ((), (), s32[]{:S(2)}) async-start(), calls=%async_computation.15 | async-start | bytes 5242880 | tf_op jit(solution)/shard_map/psum | solution.py:173
  10.8 69.9 %copy-start = (bf16[512,1024]{1,0:T(8,128)(2,1)S(1)}, bf16[512,1024]{1,0:T(8,128)(2,1)}, u32[]{:S(2)}) copy-start(bf16[512,1024]{1,0:T(8,128)(2,1)} %param.14) | copy-start | bytes 3145732
  10.8 69.9 %copy-start.29 = (f32[1024]{0:T(1024)S(1)}, f32[1024]{0:T(1024)}, u32[]{:S(2)}) copy-start(f32[1024]{0:T(1024)} %param.16) | copy-start | bytes 12292
  13.0 85.4 %copy-start.31 = (f32[512]{0:T(512)}, f32[512]{0:T(512)S(1)}, u32[]{:S(2)}) copy-start(f32[512]{0:T(512)S(1)} %get-tuple-element.140) | copy-start | bytes 6148
  45.1 44.7 %copy-start.24 = (f32[2,256,16]{1,2,0:T(8,128)}, f32[2,256,16]{1,2,0:T(8,128)S(1)}, u32[]{:S(2)}) copy-start(f32[2,256,16]{1,2,0:T(8,128)S(1)} %bitcast_bitcast_fusion.1) | copy-start | bytes 98308
  45.3 140.3 %copy-start.35 = (f32[2,16]{1,0:T(2,128)}, f32[2,16]{1,0:T(2,128)S(1)}, u32[]{:S(2)}) copy-start(f32[2,16]{1,0:T(2,128)S(1)} %slice_reduce_fusion.2) | copy-start | bytes 388
  46.7 100.5 %copy-start.37 = (f32[512]{0:T(512)}, f32[512]{0:T(512)S(1)}, u32[]{:S(2)}) copy-start(f32[512]{0:T(512)S(1)} %mul.547) | copy-start | bytes 6148
  224.0 123.7 %all-reduce.30.cloned.1.call-start = ((), (), s32[]{:S(2)}) async-start(), calls=%async_computation.8 | async-start | bytes 4194304 | tf_op jit(solution)/shard_map/psum | solution.py:125
  227.9 54.6 %copy-start.13 = (f32[512,256]{1,0:T(8,128)S(1)}, f32[512,256]{1,0:T(8,128)}, u32[]{:S(2)}) copy-start(f32[512,256]{1,0:T(8,128)} %copy-done.12) | copy-start | bytes 1572868
  227.9 56.2 %copy-start.60 = (f32[256,1]{0,1:T(1,128)S(1)}, f32[256,1]{0,1:T(1,128)}, u32[]{:S(2)}) copy-start(f32[256,1]{0,1:T(1,128)} %copy-done.59) | copy-start | bytes 3076
  227.9 56.2 %copy-start.62 = (f32[256,1]{0,1:T(1,128)S(1)}, f32[256,1]{0,1:T(1,128)}, u32[]{:S(2)}) copy-start(f32[256,1]{0,1:T(1,128)} %copy-done.61) | copy-start | bytes 3076
  227.9 56.2 %copy-start.64 = (f32[256,1]{0,1:T(1,128)S(1)}, f32[256,1]{0,1:T(1,128)}, u32[]{:S(2)}) copy-start(f32[256,1]{0,1:T(1,128)} %copy-done.63) | copy-start | bytes 3076
  227.9 56.2 %copy-start.66 = (f32[256,1]{0,1:T(1,128)S(1)}, f32[256,1]{0,1:T(1,128)}, u32[]{:S(2)}) copy-start(f32[256,1]{0,1:T(1,128)} %copy-done.65) | copy-start | bytes 3076
  228.0 188.1 %reduce-scatter.10.cloned.1.call-start = ((), (), s32[]{:S(2)}) async-start(), calls=%async_computation.12 | async-start | bytes 1179648 | tf_op jit(solution)/shard_map/reduce_scatter | solution.py:196
  286.5 152.2 %all-reduce.32.cloned.1.call-start = ((), (), s32[]{:S(2)}) async-start(), calls=%async_computation.9 | async-start | bytes 4194304 | tf_op jit(solution)/shard_map/psum | solution.py:125
  347.7 150.6 %reduce-scatter.12.cloned.1.call-start = ((), (), s32[]{:S(2)}) async-start(), calls=%async_computation.13 | async-start | bytes 73728 | tf_op jit(solution)/shard_map/reduce_scatter | solution.py:197
  348.8 221.5 %reduce-scatter.14.cloned.1.call-start = ((), (), s32[]{:S(2)}) async-start(), calls=%async_computation.14 | async-start | bytes 2359296 | tf_op jit(solution)/shard_map/reduce_scatter | solution.py:198
  352.3 289.9 %reduce-scatter.8.cloned.1.call-start = ((), (), s32[]{:S(2)}) async-start(), calls=%async_computation.11 | async-start | bytes 2359296 | tf_op jit(solution)/shard_map/reduce_scatter | solution.py:190
  355.5 359.0 %reduce-scatter.6.cloned.1.call-start = ((), (), s32[]{:S(2)}) async-start(), calls=%async_computation.10 | async-start | bytes 2359296 | tf_op jit(solution)/shard_map/reduce_scatter | solution.py:184
  358.0 80.6 %copy-start.67 = (f32[512]{0:T(512)S(1)}, f32[512]{0:T(512)}, u32[]{:S(2)}) copy-start(f32[512]{0:T(512)} %get-tuple-element.139) | copy-start | bytes 6148
  (64 other events, 744.1 us)
Sparse Core Ops, SparseCore 0:
  10.1 43.4 all-gather.3
  55.7 39.5 all-gather.5
  97.3 38.3 all-gather.7
  224.1 58.3 all-reduce.33
  284.6 63.0 all-reduce.29
  351.5 64.4 reduce-scatter.9
  418.4 20.1 all-reduce.31
  442.3 55.9 reduce-scatter.11
  502.4 67.9 reduce-scatter.13
  574.3 67.8 reduce-scatter.7
  646.3 68.1 reduce-scatter.5
